TPU v7x, 256 devices: a whole 4x4x8 slice. The times are simulated.
256 devices in a mesh: hid: 32 (over z, y), wid: 8 (over x, core).
Axes of the slice: x: 4, y: 4, z: 8, core: 2. Of those that a mesh axis runs over, the one named last changes fastest.
Arguments:
- inputs: bfloat16 [256, 12288], P(None, 'wid'), may hold values from -6 to 6
- gate_pre: bfloat16 [256, 32768], P(None, 'hid'), may hold values from -8 to 8
- up_pre: bfloat16 [256, 32768], P(None, 'hid'), may hold values from -6 to 6
- out_grad: bfloat16 [256, 12288], P(None, 'wid'), may hold values from -6 to 6
- gate_codes: int32 [6144, 32768], P('wid', 'hid'), may hold values from 0 to 255
- up_codes: int32 [6144, 32768], P('wid', 'hid'), may hold values from 0 to 255
- down_codes: int32 [16384, 12288], P('hid', 'wid'), may hold values from 0 to 255
- gate_scale: float32 [96, 32768], P('wid', 'hid'), may hold values from 0.0010825318 to 0.0027063293
- up_scale: float32 [96, 32768], P('wid', 'hid'), may hold values from 0.0010825318 to 0.0027063293
- down_scale: float32 [256, 12288], P('hid', 'wid'), may hold values from 0.0006629126 to 0.0016572815
Outputs:
- input_grad: bfloat16 [256, 12288], P('hid', 'wid')
- gate_log_grad: float32 [96, 32768], P('wid', 'hid')
- up_log_grad: float32 [96, 32768], P('wid', 'hid')
- down_log_grad: float32 [256, 12288], P('hid', 'wid')
Inputs may be any that keep to these rules, and one draw needn't show every extreme that they name: `gate_codes`: each word holds two independent four-bit codes. `up_codes`: each word holds two independent four-bit codes. `down_codes`: each word holds two independent four-bit codes.
All inputs are finite; a program needn't handle non-finite values.
Results may differ from a plain program's by a relative error of at most 0.007.
Values may be sent and summed in bfloat16 or wider, within the bound.
A program may use at most 128 MiB of HBM per device.

v0:
```python
import jax
import jax.numpy as jnp
from jax import lax
from jax.sharding import PartitionSpec as P

HB = 4096
GROUP = 128


def from_partner(value, axis, bit):
    mask = 2**bit
    pairs = [(source, source ^ mask) for source in range(lax.axis_size(axis))]
    return lax.ppermute(value, axis, pairs)


def unpack_centred(packed):
    shifts = 4 * jnp.arange(2, dtype=jnp.int32)
    nibbles = jnp.bitwise_and(jnp.right_shift(packed[:, None, :], shifts[None, :, None]), 15)
    nibbles = nibbles.reshape(packed.shape[0] * 2, packed.shape[1])
    return (nibbles - 8).astype(jnp.float32)


def dequantize(packed, scales):
    centred = unpack_centred(packed)
    weight = (centred * jnp.repeat(scales, GROUP, axis=0)).astype(jnp.bfloat16)
    return (weight, centred)


def signs_table(extent):
    indices = jnp.arange(extent, dtype=jnp.int32)
    common_bits = jnp.bitwise_and(indices[:, None], indices[None, :])
    parity = jnp.zeros((extent, extent), jnp.int32)
    for bit_index in range(extent.bit_length() - 1):
        parity = parity + jnp.bitwise_and(jnp.right_shift(common_bits, bit_index), 1)
    return (1 - 2 * (parity % 2)).astype(jnp.bfloat16)


def group_sum(values, centred, scales):
    height, across = values.shape
    return scales * (centred * values).reshape(height // GROUP, GROUP, across).sum(axis=1)


def shards(
    inputs,
    gate_pre,
    up_pre,
    out_grad,
    gate_codes,
    up_codes,
    down_codes,
    gate_scale,
    up_scale,
    down_scale,
):
    hid_width = gate_pre.shape[1]
    gate_weight, gate_centred = dequantize(gate_codes, gate_scale)
    up_weight, up_centred = dequantize(up_codes, up_scale)
    down_weight, down_centred = dequantize(down_codes, down_scale)
    partial_value = lax.dot_general(
        out_grad, down_weight, (((1,), (1,)), ((), ())), preferred_element_type=jnp.float32
    )
    summed = lax.psum(partial_value, "wid")
    rotated_grad = summed.astype(jnp.bfloat16)
    gate_val = gate_pre.astype(jnp.float32)
    up_val = up_pre.astype(jnp.float32)
    activated = jax.nn.silu(gate_val)
    hidden = (activated * up_val).astype(jnp.bfloat16)
    signs = signs_table(hid_width)
    turn_fwd = jnp.dot(hidden, signs, preferred_element_type=jnp.float32)
    turn_back = jnp.dot(rotated_grad, signs, preferred_element_type=jnp.float32)
    position = lax.axis_index("hid")
    for bit_index in range((HB // hid_width).bit_length() - 1):
        far_fwd, far_back = from_partner((turn_fwd, turn_back), "hid", bit_index)
        upper_half = jnp.bitwise_and(jnp.right_shift(position, bit_index), 1) == 1
        turn_fwd = jnp.where(upper_half, far_fwd - turn_fwd, turn_fwd + far_fwd)
        turn_back = jnp.where(upper_half, far_back - turn_back, turn_back + far_back)
    scaling = HB ** (-0.5)
    rotated = (turn_fwd * scaling).astype(jnp.bfloat16)
    hidden_grad = turn_back * scaling
    sigmoid_gate = jax.nn.sigmoid(gate_val)
    slope = sigmoid_gate * (1.0 + gate_val * (1.0 - sigmoid_gate))
    gate_grad = (hidden_grad * up_val * slope).astype(jnp.bfloat16)
    up_grad = (hidden_grad * activated).astype(jnp.bfloat16)
    contract = (((1,), (1,)), ((), ()))
    first_term = lax.dot_general(
        gate_grad, gate_weight, contract, preferred_element_type=jnp.float32
    )
    grad_inputs = lax.psum_scatter(
        first_term
        + lax.dot_general(up_grad, up_weight, contract, preferred_element_type=jnp.float32),
        "hid",
        scatter_dimension=0,
        tiled=True,
    ).astype(jnp.bfloat16)
    token_contract = (((0,), (0,)), ((), ()))
    gate_full = lax.dot_general(
        inputs, gate_grad, token_contract, preferred_element_type=jnp.float32
    )
    gate_log_grad = group_sum(gate_full, gate_centred, gate_scale)
    up_full = lax.dot_general(inputs, up_grad, token_contract, preferred_element_type=jnp.float32)
    up_log_grad = group_sum(up_full, up_centred, up_scale)
    down_full = lax.dot_general(
        rotated, out_grad, token_contract, preferred_element_type=jnp.float32
    )
    down_log_grad = group_sum(down_full, down_centred, down_scale)
    return (grad_inputs, gate_log_grad, up_log_grad, down_log_grad)


def solution(mesh):
    in_specs = (
        P(None, "wid"),
        P(None, "hid"),
        P(None, "hid"),
        P(None, "wid"),
        P("wid", "hid"),
        P("wid", "hid"),
        P("hid", "wid"),
        P("wid", "hid"),
        P("wid", "hid"),
        P("hid", "wid"),
    )
    out_specs = (P("hid", "wid"), P("wid", "hid"), P("wid", "hid"), P("hid", "wid"))
    return jax.shard_map(shards, mesh=mesh, in_specs=in_specs, out_specs=out_specs, check_vma=False)
```

profile of v0, /device:TPU:6, one launch (start us, length us, event | category | flops | bytes accessed | tf_op | source)
XLA Modules:
  0.0 427.3 jit_solution(3155021112805887350)
XLA Ops:
  7.4 6.8 %shift_right_arithmetic.142 = s32[512,2,1536]{2,1,0:T(2,128)} broadcast(s32[512,1536]{1,0:T(8,128)} %param.16), dimensions={0,2} | broadcast | bytes 9437184 | tf_op jit(solution)/shard_map/shift_right_arithmetic | solution.py:18
  14.3 8.4 %shift_right_arithmetic.143 = s32[1024,1536]{1,0:T(8,128)} reshape(s32[512,2,1536]{2,1,0:T(2,128)} %shift_right_arithmetic.142) | data formatting | bytes 12582912 | tf_op jit(solution)/shard_map/shift_right_arithmetic | solution.py:18
  22.7 3.6 fusion
  27.3 48.8 %all-reduce.1 = bf16[256,1024]{0,1:T(8,128)(2,1)S(1)} all-reduce(f32[256,1024]{0,1:T(8,128)S(1)} %convolution_bitcast_fusion), channel_id=1, replica_groups=mesh['hid'=32,'wid'=8] {'wid'}, use_global_device_ids=true, to_apply=%region_0.0 | all-reduce | flops 262144 | bytes 1572864 | tf_op jit(solution)/shard_map/psum | solution.py:62
  76.2 6.8 %fusion.16 = f32[256,1024]{1,0:T(8,128)S(1)} fusion(bf16[256,1024]{0,1:T(8,128)(2,1)S(1)} %all-reduce.1), kind=kOutput, calls=%fused_computation.28 | convolution fusion | flops 583008256 | bytes 1572864 | tf_op jit(solution)/shard_map/dot_general | solution.py:70
  84.7 22.1 %collective-permute-done = f32[256,1024]{1,0:T(8,128)} collective-permute-done((f32[256,1024]{1,0:T(8,128)S(1)}, f32[256,1024]{1,0:T(8,128)}, u32[]{:S(2)}, u32[]{:S(2)}) %collective-permute-start) | collective-permute-done | bytes 1048608 | tf_op jit(solution)/shard_map/ppermute | solution.py:13
  108.3 4.9 %collective-permute-start.1 = (f32[256,1024]{1,0:T(8,128)S(1)}, f32[256,1024]{1,0:T(8,128)}, u32[]{:S(2)}, u32[]{:S(2)}) collective-permute-start(f32[256,1024]{1,0:T(8,128)S(1)} %add_select_fusion.2), channel_id=1, source_target_pairs={{0,16},{8,24},{16,0},{24,8},{32,48},{40,56},{48,32},{56,40},{64,80... | collective-permute-start | bytes 3145736 | tf_op jit(solution)/shard_map/ppermute | solution.py:13
  113.2 8.7 %fusion.14 = f32[256,1024]{1,0:T(8,128)} fusion(bf16[256,1024]{1,0:T(8,128)(2,1)} %param.12, bf16[256,1024]{1,0:T(8,128)(2,1)S(1)} %copy-done.1), kind=kOutput, calls=%fused_computation.27 | convolution fusion | flops 585105408 | bytes 2097152 | tf_op jit(solution)/shard_map/dot_general | solution.py:69
  122.8 6.7 %shift_right_arithmetic.166 = s32[768,2,1024]{2,1,0:T(2,128)} broadcast(s32[768,1024]{1,0:T(8,128)} %param.14), dimensions={0,2} | broadcast | bytes 9437184 | tf_op jit(solution)/shard_map/shift_right_arithmetic | solution.py:18
  129.5 8.5 %shift_right_arithmetic.167 = s32[1536,1024]{1,0:T(8,128)} reshape(s32[768,2,1024]{2,1,0:T(2,128)} %shift_right_arithmetic.166) | data formatting | bytes 12582912 | tf_op jit(solution)/shard_map/shift_right_arithmetic | solution.py:18
  138.0 6.5 %copy.18 = s32[1536,1024]{0,1:T(8,128)} copy(s32[1536,1024]{1,0:T(8,128)} %shift_right_arithmetic.167) | data formatting | bytes 12582912 | tf_op jit(solution)/shard_map/shift_right_arithmetic | solution.py:18
  144.5 6.7 %shift_right_arithmetic.172 = s32[768,2,1024]{2,1,0:T(2,128)} broadcast(s32[768,1024]{1,0:T(8,128)} %param.15), dimensions={0,2} | broadcast | bytes 9437184 | tf_op jit(solution)/shard_map/shift_right_arithmetic | solution.py:18
  151.2 8.5 %shift_right_arithmetic.173 = s32[1536,1024]{1,0:T(8,128)} reshape(s32[768,2,1024]{2,1,0:T(2,128)} %shift_right_arithmetic.172) | data formatting | bytes 12582912 | tf_op jit(solution)/shard_map/shift_right_arithmetic | solution.py:18
  159.7 6.6 %copy.20 = s32[1536,1024]{0,1:T(8,128)} copy(s32[1536,1024]{1,0:T(8,128)} %shift_right_arithmetic.173) | data formatting | bytes 12582912 | tf_op jit(solution)/shard_map/shift_right_arithmetic | solution.py:18
  166.3 3.5 broadcast_in_dim.7
  169.8 6.6 %copy.19 = f32[1536,1024]{0,1:T(8,128)} copy(f32[1536,1024]{1,0:T(8,128)} %bitcast.34) | data formatting | bytes 12582912 | tf_op jit(solution)/shard_map/reshape | solution.py:25
  176.4 3.5 broadcast_in_dim.8
  179.9 6.6 %copy.21 = f32[1536,1024]{0,1:T(8,128)} copy(f32[1536,1024]{1,0:T(8,128)} %bitcast.35) | data formatting | bytes 12582912 | tf_op jit(solution)/shard_map/reshape | solution.py:25
  186.5 2.2 multiply_convert_fusion.7
  188.7 6.3 %fusion.5 = f32[256,1536]{1,0:T(8,128)S(1)} fusion(bf16[256,1024]{1,0:T(8,128)(2,1)S(1)} %get-tuple-element.5, f32[1536,1024]{0,1:T(8,128)} %copy.19, s32[1536,1024]{0,1:T(8,128)} %copy.18, s32[1536]{0:T(1024)S(1)} %shift_right_arithmetic.169), kind=kOutput, calls=%fused_computation.18 | convolution fusion | flops 814743552 | bytes 14686208 | tf_op jit(solution)/shard_map/dot_general | solution.py:85
  195.8 2.8 fusion.13
  198.7 1.9 add_select_fusion.1
  200.6 1.8 collective-permute-start.3
  202.4 26.1 %collective-permute-done.3 = f32[256,1024]{1,0:T(8,128)S(1)} collective-permute-done((f32[256,1024]{1,0:T(8,128)S(1)}, f32[256,1024]{1,0:T(8,128)S(1)}, u32[]{:S(2)}, u32[]{:S(2)}) %collective-permute-start.3) | collective-permute-done | bytes 1048608 | tf_op jit(solution)/shard_map/ppermute | solution.py:13
  228.4 4.1 bitcast_reduce_fusion
  233.2 3.8 bitcast_multiply_fusion
  237.0 6.6 %copy.23 = f32[1536,1024]{1,0:T(8,128)} copy(f32[1536,1024]{0,1:T(8,128)} %bitcast_multiply_fusion) | data formatting | bytes 12582912 | tf_op jit(solution)/shard_map/mul | solution.py:40
  243.6 3.5 reduce_sum.28
  247.8 6.6 %bitcast_multiply_fusion.1 = f32[1536,1024]{0,1:T(8,128)} fusion(s32[1536,1024]{0,1:T(8,128)} %copy.18, bf16[256,1024]{1,0:T(8,128)(2,1)S(1)} %get-tuple-element.5, bf16[256,1536]{1,0:T(8,128)(2,1)S(1)} %copy-done, s32[1536]{0:T(1024)S(1)} %shift_right_arithmetic.169), kind=kOutput, calls=%fused_computation.2 | convolution fusion | flops 813170688 | bytes 13899776 | tf_op jit(solution)/shard_map/dot_general | solution.py:96
  254.4 6.6 %copy.22 = f32[1536,1024]{1,0:T(8,128)} copy(f32[1536,1024]{0,1:T(8,128)} %bitcast_multiply_fusion.1) | data formatting | bytes 12582912 | tf_op jit(solution)/shard_map/mul | solution.py:40
  261.0 3.5 reduce_sum.27
  265.1 153.9 %reduce-scatter.2.cloned.1.call-done = f32[8,1536]{1,0:T(8,128)} async-done(((f32[256,1536]{1,0:T(8,128)}), f32[8,1536]{1,0:T(8,128)}) %reduce-scatter.2.cloned.1.call-update) | async-done | bytes 49168 | tf_op jit(solution)/shard_map/reduce_scatter | solution.py:88
  (46 shorter events, 9.4 us)
Async XLA Ops:
  7.2 226.0 %copy-start = (bf16[256,1536]{1,0:T(8,128)(2,1)S(1)}, bf16[256,1536]{1,0:T(8,128)(2,1)}, u32[]{:S(2)}) copy-start(bf16[256,1536]{1,0:T(8,128)(2,1)} %param.10) | copy-start | bytes 2359300
  7.2 411.9 %reduce-scatter.2.cloned.1.call-start = ((), (), s32[]{:S(2)}) async-start(), calls=%async_computation.1 | async-start | bytes 1622016 | tf_op jit(solution)/shard_map/reduce_scatter | solution.py:88
  14.3 8.4 %copy-start.4 = (f32[8,1536]{1,0:T(8,128)S(1)}, f32[8,1536]{1,0:T(8,128)}, u32[]{:S(2)}) copy-start(f32[8,1536]{1,0:T(8,128)} %param.19) | copy-start | bytes 147460
  22.7 3.6 copy-start.6
  76.2 37.0 %copy-start.1 = (bf16[256,1024]{1,0:T(8,128)(2,1)S(1)}, bf16[256,1024]{1,0:T(8,128)(2,1)}, u32[]{:S(2)}) copy-start(bf16[256,1024]{1,0:T(8,128)(2,1)} %param.11) | copy-start | bytes 1572868
  83.0 23.8 %collective-permute-start = (f32[256,1024]{1,0:T(8,128)S(1)}, f32[256,1024]{1,0:T(8,128)}, u32[]{:S(2)}, u32[]{:S(2)}) collective-permute-start(f32[256,1024]{1,0:T(8,128)S(1)} %fusion.16), channel_id=1, source_target_pairs={{0,8},{8,0},{16,24},{24,16},{32,40},{40,32},{48,56},{56,48},{64,72... | collective-permute-start | bytes 3145736 | tf_op jit(solution)/shard_map/ppermute | solution.py:13
  108.3 78.3 %collective-permute-start.1 = (f32[256,1024]{1,0:T(8,128)S(1)}, f32[256,1024]{1,0:T(8,128)}, u32[]{:S(2)}, u32[]{:S(2)}) collective-permute-start(f32[256,1024]{1,0:T(8,128)S(1)} %add_select_fusion.2), channel_id=1, source_target_pairs={{0,16},{8,24},{16,0},{24,8},{32,48},{40,56},{48,32},{56,40},{64,80... | collective-permute-start | bytes 3145736 | tf_op jit(solution)/shard_map/ppermute | solution.py:13
  121.9 76.8 %collective-permute-start.2 = (f32[256,1024]{1,0:T(8,128)}, f32[256,1024]{1,0:T(8,128)}, u32[]{:S(2)}, u32[]{:S(2)}) collective-permute-start(f32[256,1024]{1,0:T(8,128)} %fusion.14), channel_id=1, source_target_pairs={{0,8},{8,0},{16,24},{24,16},{32,40},{40,32},{48,56},{56,48},{64,72... | collective-permute-start | bytes 3145736 | tf_op jit(solution)/shard_map/ppermute | solution.py:13
  159.7 6.6 %copy-start.3 = (f32[12,1024]{1,0:T(8,128)S(1)}, f32[12,1024]{1,0:T(8,128)}, u32[]{:S(2)}) copy-start(f32[12,1024]{1,0:T(8,128)} %param.17) | copy-start | bytes 147460
  169.8 6.6 %copy-start.2 = (f32[12,1024]{1,0:T(8,128)S(1)}, f32[12,1024]{1,0:T(8,128)}, u32[]{:S(2)}) copy-start(f32[12,1024]{1,0:T(8,128)} %param.18) | copy-start | bytes 147460
  186.5 8.5 %slice-start.4 = ((s8[6291456]{0:T(1024)(128)(4,1)}), s8[4194304]{0:T(1024)(128)(4,1)S(1)}, s32[]{:S(2)}) async-start(s8[6291456]{0:T(1024)(128)(4,1)} %bitcast.30), calls=%async_computation.6 | async-start | bytes 8388608
  188.7 6.3 %slice-start = ((s8[6291456]{0:T(1024)(128)(4,1)}), s8[4194304]{0:T(1024)(128)(4,1)S(1)}, s32[]{:S(2)}) async-start(s8[6291456]{0:T(1024)(128)(4,1)} %bitcast.26), calls=%async_computation.2 | async-start | bytes 8388608
  188.7 6.5 %slice-start.1 = ((s8[6291456]{0:T(1024)(128)(4,1)}), s8[2097152]{0:T(1024)(128)(4,1)S(1)}, s32[]{:S(2)}) async-start(s8[6291456]{0:T(1024)(128)(4,1)} %bitcast.26), calls=%async_computation.3 | async-start | bytes 4194304
  188.7 7.1 %slice-start.5 = ((s8[6291456]{0:T(1024)(128)(4,1)}), s8[2097152]{0:T(1024)(128)(4,1)S(1)}, s32[]{:S(2)}) async-start(s8[6291456]{0:T(1024)(128)(4,1)} %bitcast.30), calls=%async_computation.7 | async-start | bytes 4194304
  198.7 34.5 %slice-start.2 = ((s8[6291456]{0:T(1024)(128)(4,1)}), s8[4194304]{0:T(1024)(128)(4,1)S(1)}, s32[]{:S(2)}) async-start(s8[6291456]{0:T(1024)(128)(4,1)} %bitcast.28), calls=%async_computation.4 | async-start | bytes 8388608
  200.6 32.0 %copy-start.5 = (f32[8,1536]{1,0:T(8,128)S(1)}, f32[8,1536]{1,0:T(8,128)}, u32[]{:S(2)}) copy-start(f32[8,1536]{1,0:T(8,128)} %param.19) | copy-start | bytes 147460
  200.6 32.6 %slice-start.3 = ((s8[6291456]{0:T(1024)(128)(4,1)}), s8[2097152]{0:T(1024)(128)(4,1)S(1)}, s32[]{:S(2)}) async-start(s8[6291456]{0:T(1024)(128)(4,1)} %bitcast.28), calls=%async_computation.5 | async-start | bytes 4194304
  200.6 27.9 %collective-permute-start.3 = (f32[256,1024]{1,0:T(8,128)S(1)}, f32[256,1024]{1,0:T(8,128)S(1)}, u32[]{:S(2)}, u32[]{:S(2)}) collective-permute-start(f32[256,1024]{1,0:T(8,128)S(1)} %add_select_fusion.1), channel_id=1, source_target_pairs={{0,16},{8,24},{16,0},{24,8},{32,48},{40,56},{48,32},{56,40},{64,80... | collective-permute-start | bytes 3145736 | tf_op jit(solution)/shard_map/ppermute | solution.py:13
Sparse Core Ops, SparseCore 0:
  198.8 220.2 reduce-scatter.1
where the time goes:
time: 429 us; the launch traced here: 427 us
  waiting for transfers between devices  202 us (47%)
  local copies, waits for them, and re-layouts  93.4 us (22%)
  blocking collectives  48.8 us (11%)
  matrix products  40.2 us (9%)
  other arithmetic  19.4 us (5%)
  between operations  14.2 us (3%)
  starting transfers between devices  9.06 us (2%)
    reduce_scatter x1, waiting for transfers between devices, shards(): lax.psum_scatter(first_term + lax.dot_general(up_grad, up_weight, contrac...  154 us
    shift_right_arithmetic x12, local copies, waits for them, and re-layouts, unpack_centred(): jnp.right_shift(packed[:, None, :], shifts[None, :, None])  59.2 us
    psum x1, blocking collectives, shards(): summed = lax.psum(partial_value, 'wid')  48.8 us
    ppermute x4, waiting for transfers between devices, from_partner(): return lax.ppermute(value, axis, pairs)  48.2 us
    reshape x2, local copies, waits for them, and re-layouts, dequantize(): weight = (centred * jnp.repeat(scales, GROUP, axis=0)).astype(jnp.bfloat16)  13.2 us
    mul x2, local copies, waits for them, and re-layouts, group_sum(): centred * values  13.2 us
    ppermute x4, starting transfers between devices, from_partner(): return lax.ppermute(value, axis, pairs)  9.02 us
    dot_general x1, matrix products, shards(): turn_fwd = jnp.dot(hidden, signs, preferred_element_type=jnp.float32)  8.72 us
  transfers between devices with their start and end apart: 5, of which 3 were waited for; matrix products, arithmetic and copies ran while one was open for 29% of the time, Pallas kernels for 0%

commit v1 on v0

--- a/solution.py
+++ b/solution.py
@@ -59,7 +59,7 @@
     partial_value = lax.dot_general(
         out_grad, down_weight, (((1,), (1,)), ((), ())), preferred_element_type=jnp.float32
     )
-    summed = lax.psum(partial_value, "wid")
+    summed = jnp.sum(lax.all_gather(partial_value, "wid"), axis=0)
     rotated_grad = summed.astype(jnp.bfloat16)
     gate_val = gate_pre.astype(jnp.float32)
     up_val = up_pre.astype(jnp.float32)

time: 429 us -> 448 us (1.044)
  waiting for transfers between devices: 202 us -> 256 us
  blocking collectives: 48.8 us -> 0 us
  local copies, waits for them, and re-layouts: 93.4 us -> 100 us
    all_gather x0 -> x1, waiting for transfers between devices: none -> 53.1 us  [shards(): summed = jnp.sum(lax.all_gather(partial_value, 'wid'), axis=0)]
    psum x1 -> x0, blocking collectives: 48.8 us -> none  [shards(): summed = lax.psum(partial_value, 'wid')]
    unnamed x26 -> x27, local copies, waits for them, and re-layouts: 0.84 us -> 8.33 us
  transfers between devices with their start and end apart: 5 -> 6, of which waited for: 3 -> 4; matrix products, arithmetic and copies ran while one was open for 29% -> 28% of each run, Pallas kernels for 0% -> 0%
where the time goes in v1:
time: 448 us; the launch traced here: 443 us
  waiting for transfers between devices  256 us (57%)
  local copies, waits for them, and re-layouts  100 us (22%)
  matrix products  41.2 us (9%)
  other arithmetic  21.9 us (5%)
  between operations  14.4 us (3%)
  starting transfers between devices  8.93 us (2%)
    reduce_scatter x1, waiting for transfers between devices, shards(): lax.psum_scatter(first_term + lax.dot_general(up_grad, up_weight, contrac...  155 us
    shift_right_arithmetic x12, local copies, waits for them, and re-layouts, unpack_centred(): jnp.right_shift(packed[:, None, :], shifts[None, :, None])  59 us
    all_gather x1, waiting for transfers between devices, shards(): summed = jnp.sum(lax.all_gather(partial_value, 'wid'), axis=0)  53.1 us
    ppermute x4, waiting for transfers between devices, from_partner(): return lax.ppermute(value, axis, pairs)  47.8 us
    reshape x2, local copies, waits for them, and re-layouts, dequantize(): weight = (centred * jnp.repeat(scales, GROUP, axis=0)).astype(jnp.bfloat16)  13.2 us
    mul x2, local copies, waits for them, and re-layouts, group_sum(): centred * values  13.2 us
  transfers between devices with their start and end apart: 6, of which 4 were waited for; matrix products, arithmetic and copies ran while one was open for 28% of the time, Pallas kernels for 0%

profile of v1, /device:TPU:6, one launch (start us, length us, event | category | flops | bytes accessed | tf_op | source)
XLA Modules:
  0.0 442.9 jit_solution(15619510519711244035)
XLA Ops:
  7.4 6.8 %shift_right_arithmetic.142 = s32[512,2,1536]{2,1,0:T(2,128)} broadcast(s32[512,1536]{1,0:T(8,128)} %param.16), dimensions={0,2} | broadcast | bytes 9437184 | tf_op jit(solution)/shard_map/shift_right_arithmetic | solution.py:18
  14.2 8.4 %shift_right_arithmetic.143 = s32[1024,1536]{1,0:T(8,128)} reshape(s32[512,2,1536]{2,1,0:T(2,128)} %shift_right_arithmetic.142) | data formatting | bytes 12582912 | tf_op jit(solution)/shard_map/shift_right_arithmetic | solution.py:18
  22.6 3.6 fusion
  28.6 53.1 %all-gather.3.cloned.1.call-done = f32[2048,1024]{0,1:T(8,128)} async-done(((f32[256,1024]{0,1:T(8,128)}), f32[2048,1024]{0,1:T(8,128)}) %all-gather.3.cloned.1.call-update) | async-done | bytes 8388624 | tf_op jit(solution)/shard_map/all_gather | solution.py:62
  81.7 7.5 %copy.30 = f32[128,8,8,256]{3,2,1,0:T(8,128)S(1)} copy(f32[128,8,8,256]{3,1,2,0:T(8,128)} %bitcast.41) | data formatting | bytes 16777216
  89.2 2.6 bitcast_reduce_fusion
  91.8 6.8 %fusion.16 = f32[256,1024]{1,0:T(8,128)S(1)} fusion(bf16[256,1024]{0,1:T(8,128)(2,1)S(1)} %bitcast_reduce_fusion), kind=kOutput, calls=%fused_computation.29 | convolution fusion | flops 583008256 | bytes 1572864 | tf_op jit(solution)/shard_map/dot_general | solution.py:70
  100.3 23.8 %collective-permute-done = f32[256,1024]{1,0:T(8,128)} collective-permute-done((f32[256,1024]{1,0:T(8,128)S(1)}, f32[256,1024]{1,0:T(8,128)}, u32[]{:S(2)}, u32[]{:S(2)}) %collective-permute-start) | collective-permute-done | bytes 1048608 | tf_op jit(solution)/shard_map/ppermute | solution.py:13
  125.5 3.5 collective-permute-start.1
  129.0 8.7 %fusion.14 = f32[256,1024]{1,0:T(8,128)} fusion(bf16[256,1024]{1,0:T(8,128)(2,1)} %param.12, bf16[256,1024]{1,0:T(8,128)(2,1)S(1)} %copy-done.1), kind=kOutput, calls=%fused_computation.28 | convolution fusion | flops 585105408 | bytes 2097152 | tf_op jit(solution)/shard_map/dot_general | solution.py:69
  139.1 6.6 %shift_right_arithmetic.166 = s32[768,2,1024]{2,1,0:T(2,128)} broadcast(s32[768,1024]{1,0:T(8,128)} %param.14), dimensions={0,2} | broadcast | bytes 9437184 | tf_op jit(solution)/shard_map/shift_right_arithmetic | solution.py:18
  145.7 8.5 %shift_right_arithmetic.167 = s32[1536,1024]{1,0:T(8,128)} reshape(s32[768,2,1024]{2,1,0:T(2,128)} %shift_right_arithmetic.166) | data formatting | bytes 12582912 | tf_op jit(solution)/shard_map/shift_right_arithmetic | solution.py:18
  154.2 6.6 %copy.24 = s32[1536,1024]{0,1:T(8,128)} copy(s32[1536,1024]{1,0:T(8,128)} %shift_right_arithmetic.167) | data formatting | bytes 12582912 | tf_op jit(solution)/shard_map/shift_right_arithmetic | solution.py:18
  160.8 6.6 %shift_right_arithmetic.172 = s32[768,2,1024]{2,1,0:T(2,128)} broadcast(s32[768,1024]{1,0:T(8,128)} %param.15), dimensions={0,2} | broadcast | bytes 9437184 | tf_op jit(solution)/shard_map/shift_right_arithmetic | solution.py:18
  167.4 8.4 %shift_right_arithmetic.173 = s32[1536,1024]{1,0:T(8,128)} reshape(s32[768,2,1024]{2,1,0:T(2,128)} %shift_right_arithmetic.172) | data formatting | bytes 12582912 | tf_op jit(solution)/shard_map/shift_right_arithmetic | solution.py:18
  175.9 6.6 %copy.26 = s32[1536,1024]{0,1:T(8,128)} copy(s32[1536,1024]{1,0:T(8,128)} %shift_right_arithmetic.173) | data formatting | bytes 12582912 | tf_op jit(solution)/shard_map/shift_right_arithmetic | solution.py:18
  182.5 3.4 broadcast_in_dim.7
  185.9 6.6 %copy.25 = f32[1536,1024]{0,1:T(8,128)} copy(f32[1536,1024]{1,0:T(8,128)} %bitcast.39) | data formatting | bytes 12582912 | tf_op jit(solution)/shard_map/reshape | solution.py:25
  192.5 3.4 broadcast_in_dim.8
  195.9 6.5 %copy.27 = f32[1536,1024]{0,1:T(8,128)} copy(f32[1536,1024]{1,0:T(8,128)} %bitcast.40) | data formatting | bytes 12582912 | tf_op jit(solution)/shard_map/reshape | solution.py:25
  204.6 6.3 %fusion.5 = f32[256,1536]{1,0:T(8,128)S(1)} fusion(bf16[256,1024]{1,0:T(8,128)(2,1)S(1)} %get-tuple-element.5, f32[1536,1024]{0,1:T(8,128)} %copy.25, s32[1536,1024]{0,1:T(8,128)} %copy.24, s32[1536]{0:T(1024)S(1)} %shift_right_arithmetic.169), kind=kOutput, calls=%fused_computation.19 | convolution fusion | flops 814743552 | bytes 14686208 | tf_op jit(solution)/shard_map/dot_general | solution.py:85
  211.7 2.8 fusion.13
  216.5 2.3 collective-permute-start.3
  218.8 24.0 %collective-permute-done.3 = f32[256,1024]{1,0:T(8,128)S(1)} collective-permute-done((f32[256,1024]{1,0:T(8,128)S(1)}, f32[256,1024]{1,0:T(8,128)S(1)}, u32[]{:S(2)}, u32[]{:S(2)}) %collective-permute-start.3) | collective-permute-done | bytes 1048608 | tf_op jit(solution)/shard_map/ppermute | solution.py:13
  242.8 4.1 bitcast_reduce_fusion.1
  247.5 3.8 bitcast_multiply_fusion
  251.4 6.6 %copy.29 = f32[1536,1024]{1,0:T(8,128)} copy(f32[1536,1024]{0,1:T(8,128)} %bitcast_multiply_fusion) | data formatting | bytes 12582912 | tf_op jit(solution)/shard_map/mul | solution.py:40
  258.0 3.5 reduce_sum.38
  262.1 6.6 %bitcast_multiply_fusion.1 = f32[1536,1024]{0,1:T(8,128)} fusion(s32[1536,1024]{0,1:T(8,128)} %copy.24, bf16[256,1024]{1,0:T(8,128)(2,1)S(1)} %get-tuple-element.5, bf16[256,1536]{1,0:T(8,128)(2,1)S(1)} %copy-done, s32[1536]{0:T(1024)S(1)} %shift_right_arithmetic.169), kind=kOutput, calls=%fused_computation.3 | convolution fusion | flops 813170688 | bytes 13899776 | tf_op jit(solution)/shard_map/dot_general | solution.py:96
  268.8 6.6 %copy.28 = f32[1536,1024]{1,0:T(8,128)} copy(f32[1536,1024]{0,1:T(8,128)} %bitcast_multiply_fusion.1) | data formatting | bytes 12582912 | tf_op jit(solution)/shard_map/mul | solution.py:40
  275.3 3.5 reduce_sum.37
  279.5 155.0 %reduce-scatter.2.cloned.1.call-done = f32[8,1536]{1,0:T(8,128)} async-done(((f32[256,1536]{1,0:T(8,128)}), f32[8,1536]{1,0:T(8,128)}) %reduce-scatter.2.cloned.1.call-update) | async-done | bytes 49168 | tf_op jit(solution)/shard_map/reduce_scatter | solution.py:88
  (50 shorter events, 15.2 us)
Async XLA Ops:
  7.2 240.4 %copy-start = (bf16[256,1536]{1,0:T(8,128)(2,1)S(1)}, bf16[256,1536]{1,0:T(8,128)(2,1)}, u32[]{:S(2)}) copy-start(bf16[256,1536]{1,0:T(8,128)(2,1)} %param.10) | copy-start | bytes 2359300
  7.2 74.5 %all-gather.3.cloned.1.call-start = ((), (), s32[]{:S(2)}) async-start(), calls=%async_computation.2 | async-start | bytes 9437184 | tf_op jit(solution)/shard_map/all_gather | solution.py:62
  14.2 8.4 %copy-start.4 = (f32[8,1536]{1,0:T(8,128)S(1)}, f32[8,1536]{1,0:T(8,128)}, u32[]{:S(2)}) copy-start(f32[8,1536]{1,0:T(8,128)} %param.19) | copy-start | bytes 147460
  22.6 3.6 copy-start.6
  28.3 406.2 %reduce-scatter.2.cloned.1.call-start = ((), (), s32[]{:S(2)}) async-start(), calls=%async_computation.1 | async-start | bytes 1622016 | tf_op jit(solution)/shard_map/reduce_scatter | solution.py:88
  91.7 37.3 %copy-start.1 = (bf16[256,1024]{1,0:T(8,128)(2,1)S(1)}, bf16[256,1024]{1,0:T(8,128)(2,1)}, u32[]{:S(2)}) copy-start(bf16[256,1024]{1,0:T(8,128)(2,1)} %param.11) | copy-start | bytes 1572868
  98.6 25.5 %collective-permute-start = (f32[256,1024]{1,0:T(8,128)S(1)}, f32[256,1024]{1,0:T(8,128)}, u32[]{:S(2)}, u32[]{:S(2)}) collective-permute-start(f32[256,1024]{1,0:T(8,128)S(1)} %fusion.16), channel_id=1, source_target_pairs={{0,8},{8,0},{16,24},{24,16},{32,40},{40,32},{48,56},{56,48},{64,72... | collective-permute-start | bytes 3145736 | tf_op jit(solution)/shard_map/ppermute | solution.py:13
  125.5 76.9 %collective-permute-start.1 = (f32[256,1024]{1,0:T(8,128)S(1)}, f32[256,1024]{1,0:T(8,128)}, u32[]{:S(2)}, u32[]{:S(2)}) collective-permute-start(f32[256,1024]{1,0:T(8,128)S(1)} %add_select_fusion.2), channel_id=1, source_target_pairs={{0,16},{8,24},{16,0},{24,8},{32,48},{40,56},{48,32},{56,40},{64,80... | collective-permute-start | bytes 3145736 | tf_op jit(solution)/shard_map/ppermute | solution.py:13
  137.8 76.8 %collective-permute-start.2 = (f32[256,1024]{1,0:T(8,128)}, f32[256,1024]{1,0:T(8,128)}, u32[]{:S(2)}, u32[]{:S(2)}) collective-permute-start(f32[256,1024]{1,0:T(8,128)} %fusion.14), channel_id=1, source_target_pairs={{0,8},{8,0},{16,24},{24,16},{32,40},{40,32},{48,56},{56,48},{64,72... | collective-permute-start | bytes 3145736 | tf_op jit(solution)/shard_map/ppermute | solution.py:13
  175.9 6.6 %copy-start.3 = (f32[12,1024]{1,0:T(8,128)S(1)}, f32[12,1024]{1,0:T(8,128)}, u32[]{:S(2)}) copy-start(f32[12,1024]{1,0:T(8,128)} %param.17) | copy-start | bytes 147460
  185.8 6.7 %copy-start.2 = (f32[12,1024]{1,0:T(8,128)S(1)}, f32[12,1024]{1,0:T(8,128)}, u32[]{:S(2)}) copy-start(f32[12,1024]{1,0:T(8,128)} %param.18) | copy-start | bytes 147460
  202.4 8.5 %slice-start.4 = ((s8[6291456]{0:T(1024)(128)(4,1)}), s8[4194304]{0:T(1024)(128)(4,1)S(1)}, s32[]{:S(2)}) async-start(s8[6291456]{0:T(1024)(128)(4,1)} %bitcast.35), calls=%async_computation.7 | async-start | bytes 8388608
  204.6 6.3 %slice-start = ((s8[6291456]{0:T(1024)(128)(4,1)}), s8[4194304]{0:T(1024)(128)(4,1)S(1)}, s32[]{:S(2)}) async-start(s8[6291456]{0:T(1024)(128)(4,1)} %bitcast.31), calls=%async_computation.3 | async-start | bytes 8388608
  204.6 6.5 %slice-start.1 = ((s8[6291456]{0:T(1024)(128)(4,1)}), s8[2097152]{0:T(1024)(128)(4,1)S(1)}, s32[]{:S(2)}) async-start(s8[6291456]{0:T(1024)(128)(4,1)} %bitcast.31), calls=%async_computation.4 | async-start | bytes 4194304
  204.6 7.1 %slice-start.5 = ((s8[6291456]{0:T(1024)(128)(4,1)}), s8[2097152]{0:T(1024)(128)(4,1)S(1)}, s32[]{:S(2)}) async-start(s8[6291456]{0:T(1024)(128)(4,1)} %bitcast.35), calls=%async_computation.8 | async-start | bytes 4194304
  214.6 33.0 %slice-start.2 = ((s8[6291456]{0:T(1024)(128)(4,1)}), s8[4194304]{0:T(1024)(128)(4,1)S(1)}, s32[]{:S(2)}) async-start(s8[6291456]{0:T(1024)(128)(4,1)} %bitcast.33), calls=%async_computation.5 | async-start | bytes 8388608
  216.5 30.4 %copy-start.5 = (f32[8,1536]{1,0:T(8,128)S(1)}, f32[8,1536]{1,0:T(8,128)}, u32[]{:S(2)}) copy-start(f32[8,1536]{1,0:T(8,128)} %param.19) | copy-start | bytes 147460
  216.5 31.1 %slice-start.3 = ((s8[6291456]{0:T(1024)(128)(4,1)}), s8[2097152]{0:T(1024)(128)(4,1)S(1)}, s32[]{:S(2)}) async-start(s8[6291456]{0:T(1024)(128)(4,1)} %bitcast.33), calls=%async_computation.6 | async-start | bytes 4194304
  216.5 26.3 %collective-permute-start.3 = (f32[256,1024]{1,0:T(8,128)S(1)}, f32[256,1024]{1,0:T(8,128)S(1)}, u32[]{:S(2)}, u32[]{:S(2)}) collective-permute-start(f32[256,1024]{1,0:T(8,128)S(1)} %add_select_fusion.1), channel_id=1, source_target_pairs={{0,16},{8,24},{16,0},{24,8},{32,48},{40,56},{48,32},{56,40},{64,80... | collective-permute-start | bytes 3145736 | tf_op jit(solution)/shard_map/ppermute | solution.py:13
Sparse Core Ops, SparseCore 0:
  28.4 53.2 all-gather.2
  214.7 219.7 reduce-scatter.1
